TPU v7x, 128 devices: a whole 4x4x4 slice. The times are simulated.
128 devices in a mesh: wide: 16 (over y_hi, z, core), narrow: 8 (over y_lo, x).
Axes of the slice: x: 4, y: 4 (y_hi: 2, y_lo: 2; y = y_hi * 2 + y_lo), z: 4, core: 2. Of those that a mesh axis runs over, the one named last changes fastest.
Arguments:
- inputs: bfloat16 [1, 4096, 4096], P(None, 'narrow', 'wide'), may hold values from -6 to 6
- out_cotangent: bfloat16 [1, 1, 4096, 14336], P(None, None, ('wide', 'narrow')), may hold values from -0.0014648438 to 0.0014648438
- sign_bits: int32 [1, 4096, 16384], P(None, 'wide', 'narrow'), may hold values 0 or 1
- row_pick: int32 [1, 8192], replicated, may hold values from 0 to 4095
- col_pick: int32 [1, 8192], replicated, may hold values from 0 to 16383
Outputs:
- sketch: float32 [1, 1, 8192], P(None, None, ('wide', 'narrow'))
All inputs are finite; a program needn't handle non-finite values. No bound on the sum of `sign_bits` on one device may be relied on, other than what follows from the above.
Results may differ from a plain program's by a relative error of at most 0.0003.
Values may be sent and summed in bfloat16 or wider, within the bound.
A program may use at most 128 MiB of HBM per device.

v0:
```python
import jax
import jax.numpy as jnp
from jax import lax
from jax.sharding import PartitionSpec as P


def hadamard(length):
    index = jnp.arange(length, dtype=jnp.int32)
    parity = jnp.zeros((length, length), jnp.int32)
    for bit_number in range(length.bit_length() - 1):
        parity = parity ^ index[:, None] >> bit_number & 1 & (index[None, :] >> bit_number & 1)
    return (1 - 2 * parity).astype(jnp.float32)


def transform_last(block):
    width_all = block.shape[-1]
    leading = block.ndim - 1
    factors = []
    remain = width_all
    while remain > 1:
        factor = min(128, remain)
        factors.append(factor)
        remain = remain // factor
    shaped = block.reshape(block.shape[:-1] + tuple(factors))
    for placed, factor in enumerate(factors):
        mixed = jnp.tensordot(
            shaped,
            hadamard(factor),
            axes=([leading + placed], [0]),
            precision=lax.Precision.HIGHEST,
        )
        shaped = jnp.moveaxis(mixed, -1, leading + placed)
    return shaped.reshape(block.shape)


def body(inputs, out_cotangent, sign_bits, row_pick, col_pick):
    wide_count = lax.axis_size("wide")
    narrow_count = lax.axis_size("narrow")
    row_local = inputs.shape[2]
    col_local = sign_bits.shape[2]
    hidden_all = out_cotangent.shape[3]
    padded_width = col_local * narrow_count
    whole_inputs = lax.all_gather(inputs, "narrow", axis=1, tiled=True)
    padded_cot = jnp.pad(out_cotangent, ((0, 0), (0, 0), (0, 0), (0, padded_width - hidden_all)))
    column_cot = lax.all_to_all(padded_cot, "narrow", split_axis=3, concat_axis=2, tiled=True)
    grads = jnp.einsum(
        "etr,metc->merc",
        whole_inputs,
        lax.all_gather(column_cot, "wide", axis=2, tiled=True),
        preferred_element_type=jnp.float32,
    )
    signs = (2 * sign_bits - 1).astype(jnp.float32)
    row_mix = hadamard(row_local)
    wide_index = lax.axis_index("wide")
    narrow_index = lax.axis_index("narrow")
    row_high = row_pick // row_local
    row_low = row_pick % row_local
    col_high = col_pick // col_local
    col_low = col_pick % col_local
    position = row_low * col_local + col_low
    block_len = row_local * col_local
    piece_len = block_len // (wide_count * narrow_count)
    signed = grads[:, 0] * signs
    rows_done = jnp.einsum("ij,mjc->mic", row_mix, signed, precision=lax.Precision.HIGHEST)
    local_done = transform_last(rows_done).reshape(signed.shape[0], block_len)
    pieces = local_done.reshape(signed.shape[0], wide_count * narrow_count, piece_len)
    received = lax.all_to_all(pieces, ("wide", "narrow"), split_axis=1, concat_axis=1, tiled=True)
    finished = jnp.einsum(
        "ts,msj->mtj",
        hadamard(wide_count * narrow_count),
        received,
        precision=lax.Precision.HIGHEST,
    )
    my_piece = wide_index * narrow_count + narrow_index
    target = row_high * narrow_count + col_high
    owned = position // piece_len == my_piece
    lookup = target * piece_len + position % piece_len
    picked = jnp.take_along_axis(finished.reshape(signed.shape[0], -1), lookup, axis=1)
    contributions = [jnp.where(owned, picked, jnp.float32(0.0))]
    stacked = jnp.stack(contributions)
    summed = lax.psum_scatter(stacked, ("wide", "narrow"), scatter_dimension=2, tiled=True)
    return summed / jnp.sqrt(jnp.float32(row_pick.shape[1]))


def solution(mesh):
    return jax.shard_map(
        body,
        mesh=mesh,
        in_specs=(
            P(None, "narrow", "wide"),
            P(None, None, ("wide", "narrow"), None),
            P(None, "wide", "narrow"),
            P(),
            P(),
        ),
        out_specs=P(None, None, ("wide", "narrow")),
        check_vma=False,
    )
```

profile of v0, /device:TPU:0, one launch (start us, length us, event | category | flops | bytes accessed | tf_op | source)
XLA Modules:
  0.0 1106.1 jit_solution(14091993724530731446)
XLA Ops:
  6.5 0.0 all-gather.5.cloned.1.call-start
  6.5 0.7 all-gather.5.cloned.1.call-update
  7.3 0.0 all-gather.3.cloned.1.call-start
  7.3 14.3 %copy.20 = bf16[1,1,32,14336]{2,1,0,3:T(2,128)(2,1)} copy(bf16[1,1,32,14336]{3,2,1,0:T(8,128)(2,1)} %param.6) | data formatting | bytes 1835008 | tf_op args[1]
  21.6 18.6 %pad_bitcast_fusion = bf16[16384,1,1,32]{3,2,1,0:T(2,128)(2,1)} fusion(bf16[1,1,32,14336]{2,1,0,3:T(2,128)(2,1)} %copy.20), kind=kLoop, calls=%fused_computation.160 | loop fusion | bytes 1966080
  40.2 0.5 broadcast.581
  40.7 90.8 %reduce = bf16[16384,32]{1,0:T(8,128)(2,1)} reduce(bf16[16384,1,1,32]{3,2,1,0:T(2,128)(2,1)} %pad_bitcast_fusion, bf16[]{:T(256)} %broadcast.581), dimensions={1,2}, to_apply=%pad_bitcast_fusion.reduce_sub_computation | reduce | bytes 2097154
  131.5 7.0 reshape.337
  138.4 20.9 %all_to_all.23 = bf16[8,2,32768]{2,1,0:T(2,128)(2,1)S(1)} all-to-all(bf16[8,2,32768]{2,1,0:T(2,128)(2,1)S(1)} %reshape.337), channel_id=1, replica_groups=mesh['wide'=16,'narrow'=8] {'narrow'}, dimensions={0} | all-to-all | bytes 2097152 | tf_op jit(solution)/shard_map/all_to_all | solution.py:45
  159.4 6.2 reshape.338
  165.6 15.1 %copy.21 = bf16[1,1,32,16384]{3,2,1,0:T(8,128)(2,1)S(1)} copy(bf16[1,1,32,16384]{2,1,0,3:T(2,128)(2,1)} %bitcast.73) | data formatting | bytes 2097152 | tf_op jit(solution)/shard_map/all_to_all | solution.py:45
  180.7 0.6 copy.33
  181.3 0.0 copy-start
  181.3 1.6 copy.22
  182.9 0.0 all-gather.3.cloned.1.call-update
  182.9 0.1 copy-done
  183.0 2.3 copy.23
  185.4 0.0 all-gather.5.cloned.1.call-done
  185.4 106.8 %all-gather.3.cloned.1.call-done = bf16[1,1,4096,2048]{3,2,1,0:T(8,128)(2,1)} async-done(((bf16[1,1,256,2048]{3,2,1,0:T(8,128)(2,1)}), bf16[1,1,4096,2048]{3,2,1,0:T(8,128)(2,1)}) %all-gather.3.cloned.1.call-update) | async-done | bytes 16777232 | tf_op jit(solution)/shard_map/all_gather | solution.py:49
  292.2 12.4 %fusion.8 = f32[256,2048]{0,1:T(8,128)S(1)} fusion(bf16[1,1,4096,2048]{3,2,1,0:T(8,128)(2,1)} %all-gather.3.cloned.1.call-done, bf16[1,4096,256]{2,1,0:T(8,128)(2,1)} %all-gather.5.cloned.1.call-done, s32[1,256,2048]{1,2,0:T(8,128)} %copy.23), kind=kOutput, calls=%fused_computation.6 | convolution fusion | flops 4297064448 | bytes 23068672 | tf_op jit(solution)/shard_map/etr,metc->merc/dot_general | solution.py:46
  304.6 2.2 fusion.21
  306.8 4.4 fusion.18
  311.2 29.0 %fusion.14 = f32[256,128,16]{2,1,0:T(8,128)} fusion(f32[256,128,16]{1,0,2:T(8,128)S(1)} %fusion.18, s32[16]{0:T(128)S(1)} %get-tuple-element.21, s32[16]{0:T(128)S(1)} %get-tuple-element.22, s32[16]{0:T(128)S(1)} %get-tuple-element.23, s32[16]{0:T(128)S(1)} %get-tuple-element.24), kind=kOutput, calls=%fused_computation.10 | convolution fusion | flops 100665856 | bytes 4194560 | tf_op jit(solution)/shard_map/dot_general | solution.py:26
  340.2 12.3 %reshape_reshape_reshape.4 = f32[1,128,4096]{2,0,1:T(1,128)} reshape(f32[256,128,16]{2,1,0:T(8,128)} %fusion.14) | data formatting | bytes 4194304 | tf_op jit(solution)/shard_map/reshape;reshape;reshape | solution.py:66
  352.5 0.0 copy-start.1
  352.5 0.0 copy-start.2
  352.5 6.2 all-to-all-start.1
  358.7 0.3 reduce-scatter.4.cloned.1.call-start
  359.0 0.0 copy-done.1
  359.0 0.0 copy-done.2
  359.0 0.6 compare_select_fusion
  359.7 29.0 %all-to-all-done.1 = f32[1,128,4096]{2,0,1:T(1,128)S(1)} async-done(((f32[1,128,4096]{2,0,1:T(1,128)}), f32[1,128,4096]{2,0,1:T(1,128)S(1)}, u32[]{:S(2)}, u32[]{:S(2)}) %all-to-all-start.1) | async-done | bytes 2097184 | tf_op jit(solution)/shard_map/all_to_all | solution.py:67
  388.7 5.7 convolution_bitcast_fusion
  394.3 2.9 copy.28
  397.3 2.0 copy.34
  399.2 45.5 %gather_fusion = f32[8192]{0:T(1024)S(1)} fusion(f32[524288]{0:T(1024)S(1)} %bitcast.72, s32[8192]{0:T(1024)S(1)} %broadcast_clamp_fusion), kind=kCustom, calls=%fused_computation | custom fusion | bytes 98304 | tf_op jit(solution)/shard_map/jit(take_along_axis)/gather | solution.py:78
  444.8 0.2 fusion.64
  445.0 6.3 copy.30
  451.3 0.0 reduce-scatter.4.cloned.1.call-update
  451.3 646.6 %reduce-scatter.4.cloned.1.call-done = f32[64,1]{1,0:T(8,128)} async-done(((f32[8192,1]{1,0:T(8,128)}), f32[64,1]{1,0:T(8,128)}) %reduce-scatter.4.cloned.1.call-update) | async-done | bytes 272
  1098.0 0.8 copy.31
  1098.8 0.5 broadcast_multiply_fusion
  (11 shorter events, 0.1 us)
Async XLA Ops:
  6.5 178.9 %all-gather.5.cloned.1.call-start = ((), (), s32[]{:S(2)}) async-start(), calls=%async_computation.4 | async-start | bytes 2359296 | tf_op jit(solution)/shard_map/all_gather | solution.py:43
  7.3 284.9 %all-gather.3.cloned.1.call-start = ((), (), s32[]{:S(2)}) async-start(), calls=%async_computation.3 | async-start | bytes 17825792 | tf_op jit(solution)/shard_map/all_gather | solution.py:49
  181.3 1.7 copy-start
  352.5 6.5 copy-start.1
  352.5 6.5 copy-start.2
  352.5 36.2 %all-to-all-start.1 = ((f32[1,128,4096]{2,0,1:T(1,128)}), f32[1,128,4096]{2,0,1:T(1,128)S(1)}, u32[]{:S(2)}, u32[]{:S(2)}) async-start(f32[1,128,4096]{2,0,1:T(1,128)} %reshape_reshape_reshape.4), calls=%async_computation.1 | async-start | bytes 4194304 | tf_op jit(solution)/shard_map/all_to_all | solution.py:67
  358.7 739.2 %reduce-scatter.4.cloned.1.call-start = ((), (), s32[]{:S(2)}) async-start(), calls=%async_computation.5 | async-start | bytes 4227072
Sparse Core Ops, SparseCore 0:
  9.0 43.6 all-gather.4
  183.0 109.0 all-gather.2
  451.5 646.4 reduce-scatter.3
where the time goes:
time: 1120 us; the launch traced here: 1110 us
  waiting for transfers between devices  783 us (70%)
  local copies, waits for them, and re-layouts  136 us (12%)
  other arithmetic  92.2 us (8%)
  matrix products  53.7 us (5%)
  blocking collectives  20.9 us (2%)
  between operations  13.5 us (1%)
    unnamed x4, waiting for transfers between devices  647 us
    all_gather x1, waiting for transfers between devices, body(): lax.all_gather(column_cot, 'wide', axis=2, tiled=True)  107 us
    unnamed x1, other arithmetic  90.8 us
    unnamed x16, local copies, waits for them, and re-layouts  58.7 us
    gather x1, local copies, waits for them, and re-layouts, body(): jnp.take_along_axis(finished.reshape(signed.shape[0], -1), lookup, axis=1)  45.5 us
    dot_general x2, matrix products, transform_last(): jnp.tensordot(shaped, hadamard(factor), axes=([leading + placed], [0]), p...  33.4 us
    all_to_all x1, waiting for transfers between devices, body(): lax.all_to_all(pieces, ('wide', 'narrow'), split_axis=1, concat_axis=1, t...  29 us
  transfers between devices with their start and end apart: 4, of which 3 were waited for; matrix products, arithmetic and copies ran while one was open for 14% of the time, Pallas kernels for 0%

commit v1 on v0

--- a/solution.py
+++ b/solution.py
@@ -46,7 +46,9 @@
     grads = jnp.einsum(
         "etr,metc->merc",
         whole_inputs,
-        lax.all_gather(column_cot, "wide", axis=2, tiled=True),
+        jnp.concatenate(
+            lax.all_to_all(jnp.stack([column_cot] * lax.axis_size("wide")), "wide", 0, 0), axis=2
+        ),
         preferred_element_type=jnp.float32,
     )
     signs = (2 * sign_bits - 1).astype(jnp.float32)

time: 1120 us -> 1300 us (1.16)
  waiting for transfers between devices: 783 us -> 934 us
  starting transfers between devices: 6.52 us -> 33.9 us
    all_to_all x0 -> x1, waiting for transfers between devices: none -> 217 us  [body(): lax.all_to_all(jnp.stack([column_cot] * lax.axis_size('wide')), 'wide', 0...]
    all_gather x1 -> x0, waiting for transfers between devices: 107 us -> none  [body(): lax.all_gather(column_cot, 'wide', axis=2, tiled=True)]
    all_gather x1, waiting for transfers between devices: 0.02 us -> 40.5 us  [body(): whole_inputs = lax.all_gather(inputs, 'narrow', axis=1, tiled=True)]
    all_to_all x1, starting transfers between devices: 6.23 us -> 25.6 us  [body(): lax.all_to_all(pieces, ('wide', 'narrow'), split_axis=1, concat_axis=1, t...]
    unnamed x4 -> x3, waiting for transfers between devices: 647 us -> 647 us
  transfers between devices with their start and end apart: 4 -> 4, of which waited for: 3 -> 4; matrix products, arithmetic and copies ran while one was open for 14% -> 0% of each run, Pallas kernels for 0% -> 0%
where the time goes in v1:
time: 1300 us; the launch traced here: 1290 us
  waiting for transfers between devices  934 us (72%)
  local copies, waits for them, and re-layouts  141 us (11%)
  other arithmetic  92.2 us (7%)
  matrix products  53.7 us (4%)
  starting transfers between devices  33.9 us (3%)
  blocking collectives  20.9 us (2%)
  between operations  13.8 us (1%)
    unnamed x3, waiting for transfers between devices  647 us
    all_to_all x1, waiting for transfers between devices, body(): lax.all_to_all(jnp.stack([column_cot] * lax.axis_size('wide')), 'wide', 0...  217 us
    unnamed x1, other arithmetic  90.8 us
    unnamed x16, local copies, waits for them, and re-layouts  58.6 us
    gather x1, local copies, waits for them, and re-layouts, body(): jnp.take_along_axis(finished.reshape(signed.shape[0], -1), lookup, axis=1)  45.5 us
    all_gather x1, waiting for transfers between devices, body(): whole_inputs = lax.all_gather(inputs, 'narrow', axis=1, tiled=True)  40.5 us
    dot_general x2, matrix products, transform_last(): jnp.tensordot(shaped, hadamard(factor), axes=([leading + placed], [0]), p...  33.4 us
    all_to_all x1, waiting for transfers between devices, body(): lax.all_to_all(pieces, ('wide', 'narrow'), split_axis=1, concat_axis=1, t...  29 us
  transfers between devices with their start and end apart: 4, of which 4 were waited for; matrix products, arithmetic and copies ran while one was open for 0% of the time, Pallas kernels for 0%

profile of v1, /device:TPU:0, one launch (start us, length us, event | category | flops | bytes accessed | tf_op | source)
XLA Modules:
  0.0 1289.5 jit_solution(13824541252869391909)
XLA Ops:
  6.5 14.3 %copy.20 = bf16[1,1,32,14336]{2,1,0,3:T(2,128)(2,1)} copy(bf16[1,1,32,14336]{3,2,1,0:T(8,128)(2,1)} %param.6) | data formatting | bytes 1835008 | tf_op args[1]
  20.8 18.6 %pad_bitcast_fusion = bf16[16384,1,1,32]{3,2,1,0:T(2,128)(2,1)} fusion(bf16[1,1,32,14336]{2,1,0,3:T(2,128)(2,1)} %copy.20), kind=kLoop, calls=%fused_computation.158 | loop fusion | bytes 1966080
  39.4 0.5 broadcast.583
  39.9 90.8 %reduce = bf16[16384,32]{1,0:T(8,128)(2,1)} reduce(bf16[16384,1,1,32]{3,2,1,0:T(2,128)(2,1)} %pad_bitcast_fusion, bf16[]{:T(256)} %broadcast.583), dimensions={1,2}, to_apply=%pad_bitcast_fusion.reduce_sub_computation | reduce | bytes 2097154
  130.7 7.0 reshape.344
  137.6 20.9 %all_to_all.25 = bf16[8,2,32768]{2,1,0:T(2,128)(2,1)S(1)} all-to-all(bf16[8,2,32768]{2,1,0:T(2,128)(2,1)S(1)} %reshape.344), channel_id=1, replica_groups=mesh['wide'=16,'narrow'=8] {'narrow'}, dimensions={0} | all-to-all | bytes 2097152 | tf_op jit(solution)/shard_map/all_to_all | solution.py:45
  158.6 6.2 reshape.345
  164.8 15.1 %copy.21 = bf16[1,1,32,16384]{3,2,1,0:T(8,128)(2,1)S(1)} copy(bf16[1,1,32,16384]{2,1,0,3:T(2,128)(2,1)} %bitcast.66) | data formatting | bytes 2097152 | tf_op jit(solution)/shard_map/all_to_all | solution.py:45
  179.9 0.6 copy.33
  180.5 0.6 copy.22
  181.1 6.0 stack.7
  187.1 0.0 copy-start
  187.1 7.9 all-to-all-start.1
  195.1 0.0 all-gather.2.cloned.1.call-start
  195.1 0.7 all-gather.2.cloned.1.call-update
  195.8 0.0 copy-done
  195.8 2.3 copy.23
  198.2 40.5 %all-gather.2.cloned.1.call-done = bf16[1,4096,256]{2,1,0:T(8,128)(2,1)} async-done(((bf16[1,512,256]{2,1,0:T(8,128)(2,1)}), bf16[1,4096,256]{2,1,0:T(8,128)(2,1)}) %all-gather.2.cloned.1.call-update) | async-done | bytes 2097168 | tf_op jit(solution)/shard_map/all_gather | solution.py:43
  238.7 217.1 %all-to-all-done.1 = bf16[16,1,1,256,2048]{4,3,2,1,0:T(8,128)(2,1)} async-done(((bf16[16,1,1,256,2048]{4,3,2,1,0:T(8,128)(2,1)}), bf16[16,1,1,256,2048]{4,3,2,1,0:T(8,128)(2,1)}, u32[]{:S(2)}, u32[]{:S(2)}) %all-to-all-start.1) | async-done | bytes 16777248 | tf_op jit(solution)/shard_map/all_to_all | solution.py:50
  455.8 12.4 fusion.1
  468.2 2.2 fusion.12
  470.4 4.4 fusion.9
  474.8 29.0 %fusion.5 = f32[256,128,16]{2,1,0:T(8,128)} fusion(f32[256,128,16]{1,0,2:T(8,128)S(1)} %fusion.9, s32[16]{0:T(128)S(1)} %get-tuple-element.21, s32[16]{0:T(128)S(1)} %get-tuple-element.22, s32[16]{0:T(128)S(1)} %get-tuple-element.23, s32[16]{0:T(128)S(1)} %get-tuple-element.24), kind=kOutput, calls=%fused_computation.8 | convolution fusion | flops 100665856 | bytes 4194560 | tf_op jit(solution)/shard_map/dot_general | solution.py:26
  503.8 12.3 reshape_reshape_reshape.4
  516.2 0.0 copy-start.1
  516.2 0.0 copy-start.2
  516.2 25.6 %all-to-all-start.2 = ((f32[1,128,4096]{2,0,1:T(1,128)}), f32[1,128,4096]{2,0,1:T(1,128)S(1)}, u32[]{:S(2)}, u32[]{:S(2)}) async-start(f32[1,128,4096]{2,0,1:T(1,128)} %reshape_reshape_reshape.4), calls=%async_computation.2 | async-start | bytes 4194304 | tf_op jit(solution)/shard_map/all_to_all | solution.py:69
  541.8 0.3 reduce-scatter.4.cloned.1.call-start
  542.1 0.0 copy-done.1
  542.1 0.0 copy-done.2
  542.1 0.6 compare_select_fusion
  542.7 29.0 %all-to-all-done.2 = f32[1,128,4096]{2,0,1:T(1,128)S(1)} async-done(((f32[1,128,4096]{2,0,1:T(1,128)}), f32[1,128,4096]{2,0,1:T(1,128)S(1)}, u32[]{:S(2)}, u32[]{:S(2)}) %all-to-all-start.2) | async-done | bytes 2097184 | tf_op jit(solution)/shard_map/all_to_all | solution.py:69
  571.7 5.7 convolution_bitcast_fusion
  577.4 2.9 copy.28
  580.3 2.0 copy.34
  582.3 45.5 %gather_fusion = f32[8192]{0:T(1024)S(1)} fusion(f32[524288]{0:T(1024)S(1)} %bitcast.65, s32[8192]{0:T(1024)S(1)} %broadcast_clamp_fusion), kind=kCustom, calls=%fused_computation | custom fusion | bytes 98304 | tf_op jit(solution)/shard_map/jit(take_along_axis)/gather | solution.py:80
  627.8 0.2 fusion.55
  628.0 6.3 copy.30
  634.4 0.0 reduce-scatter.4.cloned.1.call-update
  634.4 646.6 %reduce-scatter.4.cloned.1.call-done = f32[64,1]{1,0:T(8,128)} async-done(((f32[8192,1]{1,0:T(8,128)}), f32[64,1]{1,0:T(8,128)}) %reduce-scatter.4.cloned.1.call-update) | async-done | bytes 272
  1281.0 0.8 copy.31
  1281.9 0.5 broadcast_multiply_fusion
  (11 shorter events, 0.1 us)
Async XLA Ops:
  187.1 8.7 copy-start
  187.1 268.7 %all-to-all-start.1 = ((bf16[16,1,1,256,2048]{4,3,2,1,0:T(8,128)(2,1)}), bf16[16,1,1,256,2048]{4,3,2,1,0:T(8,128)(2,1)}, u32[]{:S(2)}, u32[]{:S(2)}) async-start(bf16[16,1,1,256,2048]{4,3,2,1,0:T(8,128)(2,1)} %stack.7), calls=%async_computation.1 | async-start | bytes 33554432 | tf_op jit(solution)/shard_map/all_to_all | solution.py:50
  195.1 43.7 %all-gather.2.cloned.1.call-start = ((), (), s32[]{:S(2)}) async-start(), calls=%async_computation.4 | async-start | bytes 2359296 | tf_op jit(solution)/shard_map/all_gather | solution.py:43
  516.2 25.9 %copy-start.1 = (s32[1,8192]{1,0:T(1,128)S(1)}, s32[1,8192]{1,0:T(1,128)}, u32[]{:S(2)}) copy-start(s32[1,8192]{1,0:T(1,128)} %param.9) | copy-start | bytes 98308
  516.2 25.9 %copy-start.2 = (s32[1,8192]{1,0:T(1,128)S(1)}, s32[1,8192]{1,0:T(1,128)}, u32[]{:S(2)}) copy-start(s32[1,8192]{1,0:T(1,128)} %param.8) | copy-start | bytes 98308
  516.2 55.6 %all-to-all-start.2 = ((f32[1,128,4096]{2,0,1:T(1,128)}), f32[1,128,4096]{2,0,1:T(1,128)S(1)}, u32[]{:S(2)}, u32[]{:S(2)}) async-start(f32[1,128,4096]{2,0,1:T(1,128)} %reshape_reshape_reshape.4), calls=%async_computation.2 | async-start | bytes 4194304 | tf_op jit(solution)/shard_map/all_to_all | solution.py:69
  541.8 739.2 %reduce-scatter.4.cloned.1.call-start = ((), (), s32[]{:S(2)}) async-start(), calls=%async_computation.5 | async-start | bytes 4227072
Sparse Core Ops, SparseCore 0:
  197.5 41.1 all-gather.1
  634.5 646.4 reduce-scatter.3
